TPU v7x, 32 devices: a whole 2x2x4 slice. The times are simulated.
32 devices in a mesh: dp: 8 (over z, y), tensor: 4 (over x, core).
Axes of the slice: x: 2, y: 2, z: 4, core: 2. Of those that a mesh axis runs over, the one named last changes fastest.
Arguments:
- tokens: bfloat16 [512, 1536], P('dp'), may hold values from -6 to 6
- norm_gain: float32 [1536], replicated, may hold values from 0.1 to 1.9
- w_query: bfloat16 [1536, 1024], P(None, 'tensor'), may hold values from -0.15625 to 0.15625
- w_keyval: bfloat16 [1536, 256], replicated, may hold values from -0.15625 to 0.15625
- w_out: bfloat16 [1024, 1536], P('tensor'), may hold values from -0.5 to 0.5
- kv_pool: bfloat16 [4096, 128, 256], P(('dp', 'tensor')), may hold values from -256 to 256
- page_table: int32 [512, 8], P('dp', 'tensor'), may hold values from 0 to 127, as said below
- positions: int32 [512], P('dp'), may hold values from 0 to 8191
- assignment: int32 [512], P('dp'), may hold values from 0 to 511, as said below
Outputs:
- attn_out: bfloat16 [512, 1536], P('dp')
Inputs may be any that keep to these rules, and one draw needn't show every extreme that they name: `assignment`: the serving slot is the serving device's dp index times 64 plus a local slot; each serving slot is taken by exactly one request; the 64 requests of one device go to 8 distinct devices, exactly 8 to each. `page_table`: on each device the entries form a permutation of 0 to 127.
All inputs are finite; a program needn't handle non-finite values.
Results may differ from a plain program's by a relative error of at most 0.03.
Values may be sent and summed in bfloat16 or wider, within the bound.
A program may use at most 64 MiB of HBM per device.

v0:
```python
import jax
import jax.numpy as jnp
from jax import lax
from jax.sharding import PartitionSpec as P

masked_score = -1e30
norm_eps = 1e-06
rotary_base = 10000.0


def combined_all(array, axis, join):
    gathered = jax.tree.map(
        lambda a, kind: lax.all_gather(a.astype(kind), axis),
        array,
        (jnp.bfloat16, jnp.bfloat16, jnp.bfloat16),
    )

    def take(source):
        return jax.tree.map(
            lambda a, own: lax.dynamic_index_in_dim(a, source, 0, False).astype(own.dtype),
            gathered,
            array,
        )

    return lax.fori_loop(
        1, lax.axis_size(axis), lambda source, state: join(state, take(source)), take(0)
    )


def as_sent(array):

    def short(part):
        return part.astype(jnp.bfloat16) if part.dtype == jnp.float32 else part

    return jax.tree.map(short, array)


def rotate(values, where, width):
    half = width // 2
    freqs = rotary_base ** (-jnp.arange(half, dtype=jnp.float32) * 2.0 / width)
    angles = where.astype(jnp.float32)[..., None] * freqs
    cosine = jnp.cos(angles)
    sine = jnp.sin(angles)
    first = values[..., :half]
    second = values[..., half:]
    return jnp.concatenate(
        [first * cosine - second * sine, first * sine + second * cosine], axis=-1
    )


def combine_stats(first, second):
    peak = jnp.maximum(first[0], second[0])
    first_scale = jnp.exp(first[0] - peak)
    second_scale = jnp.exp(second[0] - peak)
    total = first[1] * first_scale + second[1] * second_scale
    summed = first[2] * first_scale[..., None] + second[2] * second_scale[..., None]
    return (peak, total, summed)


def local(tokens, norm_gain, w_query, w_keyval, w_out, kv_pool, page_table, positions, assignment):
    head_width = w_keyval.shape[1] // 2
    row_count = tokens.shape[0]
    group_size = lax.axis_size("tensor")
    data_size = lax.axis_size("dp")
    local_heads = w_query.shape[1] // head_width
    all_heads = local_heads * group_size
    capacity = max(2, row_count // data_size)
    slots_all = data_size * capacity
    scale = head_width ** (-0.5)
    here = lax.axis_index("tensor")
    floats = tokens.astype(jnp.float32)
    normed = (
        floats * lax.rsqrt(jnp.mean(floats * floats, axis=-1, keepdims=True) + norm_eps) * norm_gain
    ).astype(jnp.bfloat16)
    query = jnp.dot(normed, w_query, preferred_element_type=jnp.float32).reshape(
        row_count, local_heads, head_width
    )
    query = rotate(query, positions[:, None], head_width).astype(jnp.bfloat16)
    key_value = jnp.dot(normed, w_keyval, preferred_element_type=jnp.float32)
    new_key = rotate(key_value[:, :head_width], positions, head_width).astype(jnp.bfloat16)
    new_value = key_value[:, head_width:].astype(jnp.bfloat16)
    target = assignment // row_count
    local_slot = assignment % row_count
    hits = (target[:, None] == jnp.arange(data_size, dtype=jnp.int32)[None, :]).astype(jnp.int32)
    order_in = jnp.sum(jnp.cumsum(hits, axis=0) * hits, axis=1) - 1
    place = target * capacity + order_in

    def to_buffer(values):
        empty = jnp.zeros((slots_all,) + values.shape[1:], values.dtype)
        filled = empty.at[place].set(values)
        return filled.reshape((data_size, capacity) + values.shape[1:])

    def source_buffer(values):
        return values.reshape((slots_all,) + values.shape[2:])[place]

    tags = to_buffer(jnp.stack([positions, local_slot + 1], axis=1))
    tags = lax.all_to_all(tags, "dp", split_axis=0, concat_axis=0, tiled=True).reshape(slots_all, 2)
    served_slot = tags[:, 1] - 1
    scatter_slot = jnp.where(served_slot < 0, row_count, served_slot)
    gather_slot = jnp.maximum(served_slot, 0)

    def compact(values):
        empty = jnp.zeros((row_count,) + values.shape[1:], values.dtype)
        return empty.at[scatter_slot].set(values, mode="drop")

    def expand(values):
        return values[gather_slot].reshape((data_size, capacity) + values.shape[1:])

    current = compact(tags[:, 0])
    full_query = lax.all_gather(query, "tensor", axis=1, tiled=True)
    served_heads = lax.all_to_all(
        to_buffer(full_query), "dp", split_axis=0, concat_axis=0, tiled=True
    )
    served_heads = compact(served_heads.reshape(slots_all, all_heads, head_width))
    page_rows = page_table.shape[1]
    page_len = kv_pool.shape[1]
    window = page_rows * group_size * page_len
    page_entries = kv_pool[page_table].reshape(row_count, page_rows * page_len, 2 * head_width)
    scores = (
        jnp.einsum(
            "vto,vio->vti",
            served_heads,
            page_entries[..., :head_width],
            preferred_element_type=jnp.float32,
        )
        * scale
    )
    cycle_slot = here * page_rows * page_len + jnp.arange(page_rows * page_len, dtype=jnp.int32)
    offset = jnp.mod(cycle_slot[None, :] - current[:, None], window)
    valid = ((offset != 0) & (current[:, None] - window + offset >= 0))[:, None, :]
    peak = jnp.max(jnp.where(valid, scores, masked_score), axis=2)
    weight_tensors = jnp.where(valid, jnp.exp(scores - peak[..., None]), 0.0)
    total = jnp.sum(weight_tensors, axis=2)
    summed = jnp.einsum(
        "rbi,ril->rbl",
        weight_tensors.astype(jnp.bfloat16),
        page_entries[..., head_width:],
        preferred_element_type=jnp.float32,
    )
    merged = combined_all((peak, total, summed), "tensor", combine_stats)
    returned = (
        lax.all_to_all(as_sent(expand(merged[0])), "dp", split_axis=0, concat_axis=0, tiled=True),
        lax.all_to_all(as_sent(expand(merged[1])), "dp", split_axis=0, concat_axis=0, tiled=True),
        lax.all_to_all(as_sent(expand(merged[2])), "dp", split_axis=0, concat_axis=0, tiled=True),
    )
    own_stats = tuple(
        (
            lax.dynamic_slice_in_dim(source_buffer(member), here * local_heads, local_heads, 1)
            for member in returned
        )
    )
    cache_peak, cache_total, cache_summed = own_stats
    self_score = (
        jnp.einsum("rhd,rd->rh", query, new_key, preferred_element_type=jnp.float32) * scale
    )
    overall = jnp.maximum(cache_peak, self_score)
    keep = jnp.exp(cache_peak - overall)
    fresh = jnp.exp(self_score - overall)
    full_total = cache_total * keep + fresh
    fresh_low = fresh.astype(jnp.bfloat16).astype(jnp.float32)
    full_summed = (
        cache_summed * keep[..., None]
        + fresh_low[..., None] * new_value.astype(jnp.float32)[:, None, :]
    )
    attended = (
        (full_summed / full_total[..., None])
        .astype(jnp.bfloat16)
        .reshape(row_count, local_heads * head_width)
    )
    partial_out = jnp.dot(attended, w_out, preferred_element_type=jnp.float32)
    return lax.psum(partial_out.astype(jnp.bfloat16), "tensor")


def solution(mesh):
    return jax.shard_map(
        local,
        mesh=mesh,
        in_specs=(
            P("dp", None),
            P(),
            P(None, "tensor"),
            P(),
            P("tensor", None),
            P(("dp", "tensor"), None, None),
            P("dp", "tensor"),
            P("dp"),
            P("dp"),
        ),
        out_specs=P("dp", None),
        check_vma=False,
    )
```

profile of v0, /device:TPU:0, one launch (start us, length us, event | category | flops | bytes accessed | tf_op | source)
XLA Modules:
  0.0 160.3 jit_solution(12733547716529152877)
XLA Ops:
  6.5 0.7 fusion.43
  7.3 0.7 pad_add_fusion
  8.2 0.2 select_reduce_fusion.1
  8.4 0.8 scatter_custom_fusion
  9.2 0.7 copy.68
  9.9 7.3 %all-to-all-start = ((s32[8,8,2]{1,2,0:T(2,128)}), s32[8,8,2]{1,2,0:T(2,128)S(1)}, u32[]{:S(2)}, u32[]{:S(2)}) async-start(s32[8,8,2]{1,2,0:T(2,128)} %copy.68), calls=%async_computation | async-start | bytes 16384 | tf_op jit(solution)/shard_map/all_to_all | solution.py:97
  17.2 0.7 convert_element_type.152
  17.8 1.1 fusion.15
  18.9 0.7 compare_select_fusion
  19.7 0.1 reshape.222
  19.9 1.6 fusion.25
  21.4 1.6 fusion.27
  23.2 0.2 subtract_convert_fusion.1
  23.6 0.2 fusion.32
  23.8 5.4 %all_gather.17 = bf16[64,8,128]{2,0,1:T(8,128)(2,1)S(1)} all-gather(bf16[64,2,128]{2,0,1:T(8,128)(2,1)S(1)} %pad_maximum_fusion), channel_id=1, replica_groups=mesh['dp'=8,'tensor'=4] {'tensor'}, dimensions={1}, use_global_device_ids=true | all-gather | bytes 163840 | tf_op jit(solution)/shard_map/all_gather | solution.py:110
  29.3 0.7 broadcast.188.clone
  30.0 6.9 %scatter_fusion = bf16[64,8,128]{2,1,0:T(8,128)(2,1)} fusion(bf16[64,8,128]{2,1,0:T(8,128)(2,1)} %broadcast.188.clone, s32[64]{0:T(128)S(1)} %compare_select_fusion.3, bf16[64,8,128]{2,1,0:T(8,128)(2,1)S(1)} %copy.72), kind=kCustom, calls=%fused_computation.9 | custom fusion | bytes 393472 | tf_op jit(solution)/shard_map/scatter | solution.py:90
  36.9 10.0 %gather_fusion = bf16[128,128,256]{2,1,0:T(8,128)(2,1)} fusion(bf16[128,128,256]{2,1,0:T(8,128)(2,1)} %param.16, s32[1024]{0:T(1024)S(1)} %pad_clamp_fusion.2), kind=kCustom, calls=%fused_computation | custom fusion | bytes 16777728 | tf_op jit(solution)/shard_map/gather | solution.py:118
  46.8 6.0 %all-to-all-start.1 = ((bf16[8,8,8,128]{3,2,1,0:T(8,128)(2,1)}), bf16[8,8,8,128]{3,2,1,0:T(8,128)(2,1)S(1)}, u32[]{:S(2)}, u32[]{:S(2)}) async-start(bf16[8,8,8,128]{3,2,1,0:T(8,128)(2,1)} %bitcast.9), calls=%async_computation.1 | async-start | bytes 262144 | tf_op jit(solution)/shard_map/all_to_all | solution.py:111
  52.9 0.8 scatter_custom_fusion.1
  53.8 6.5 %all-to-all-done.1 = bf16[8,8,8,128]{3,2,1,0:T(8,128)(2,1)S(1)} async-done(((bf16[8,8,8,128]{3,2,1,0:T(8,128)(2,1)}), bf16[8,8,8,128]{3,2,1,0:T(8,128)(2,1)S(1)}, u32[]{:S(2)}, u32[]{:S(2)}) %all-to-all-start.1) | async-done | bytes 131104 | tf_op jit(solution)/shard_map/all_to_all | solution.py:111
  60.3 2.5 %scatter_fusion.1 = bf16[64,8,128]{2,1,0:T(8,128)(2,1)S(1)} fusion(bf16[64,8,128]{2,1,0:T(8,128)(2,1)S(1)} %broadcast.188, s32[64]{0:T(128)S(1)} %get-tuple-element.216, bf16[64,8,128]{2,1,0:T(8,128)(2,1)S(1)} %bitcast.88), kind=kCustom, calls=%fused_computation.10 | custom fusion | bytes 393472 | tf_op jit(solution)/shard_map/scatter | solution.py:104
  62.8 3.5 %select_reduce_fusion = (f32[64,8]{1,0:T(8,128)S(1)}, f32[64,8,256]{2,1,0:T(8,128)S(1)}) fusion(pred[64,256]{1,0:T(8,128)(4,1)S(1)} %fusion.24, bf16[64,8,128]{2,1,0:T(8,128)(2,1)S(1)} %scatter_fusion.1, bf16[64,256,256]{2,1,0:T(8,128)(2,1)} %bitcast.82), kind=kOutput, calls=%fused_computation.27 | convolution fusion | flops 33947136 | bytes 4868096 | tf_op jit(solution)/shard_map/vto,vio->vti/dot_general | solution.py:120
  66.3 2.9 %fusion.10 = bf16[64,8,128]{2,1,0:T(8,128)(2,1)S(1)} fusion(bf16[64,256,256]{2,1,0:T(8,128)(2,1)} %bitcast.83, f32[64,8,256]{2,1,0:T(8,128)S(1)} %get-tuple-element.221, f32[64,8]{1,0:T(8,128)S(1)} %get-tuple-element.220, pred[64,256]{1,0:T(8,128)(4,1)S(1)} %fusion.24), kind=kOutput, calls=%fused_computation.25 | convolution fusion | flops 34013184 | bytes 4868096 | tf_op jit(solution)/shard_map/rbi,ril->rbl/dot_general | solution.py:134
  69.2 0.3 fusion.14
  69.6 5.2 %all-gather.4 = bf16[4,64,8]{1,2,0:T(8,128)(2,1)S(1)} all-gather(bf16[1,64,8]{1,2,0:T(8,128)(2,1)S(1)} %copy.75), channel_id=3, replica_groups=mesh['dp'=8,'tensor'=4] {'tensor'}, dimensions={0}, use_global_device_ids=true | all-gather | bytes 5120 | tf_op jit(solution)/shard_map/all_gather | solution.py:13
  74.8 5.1 %all-gather.3 = bf16[4,64,8]{1,2,0:T(8,128)(2,1)S(1)} all-gather(bf16[1,64,8]{1,2,0:T(8,128)(2,1)S(1)} %copy.74), channel_id=2, replica_groups=mesh['dp'=8,'tensor'=4] {'tensor'}, dimensions={0}, use_global_device_ids=true | all-gather | bytes 5120 | tf_op jit(solution)/shard_map/all_gather | solution.py:13
  79.9 7.2 %all-gather.2 = bf16[256,8,128]{2,1,0:T(8,128)(2,1)S(1)} all-gather(bf16[64,8,128]{2,1,0:T(8,128)(2,1)S(1)} %fusion.10), channel_id=4, replica_groups=mesh['dp'=8,'tensor'=4] {'tensor'}, dimensions={0}, use_global_device_ids=true | all-gather | bytes 655360 | tf_op jit(solution)/shard_map/all_gather | solution.py:13
  87.2 1.5 while.19
  87.4 0.3 fusion.58
  87.9 0.3 fusion.58
  88.4 0.3 fusion.58
  88.8 1.2 gather_fusion.3
  90.0 3.3 %all-to-all-start.3 = ((bf16[8,8,8]{2,1,0:T(8,128)(2,1)}), bf16[8,8,8]{2,1,0:T(8,128)(2,1)S(1)}, u32[]{:S(2)}, u32[]{:S(2)}) async-start(bf16[8,8,8]{2,1,0:T(8,128)(2,1)} %bitcast.65), calls=%async_computation.3 | async-start | bytes 32768 | tf_op jit(solution)/shard_map/all_to_all | solution.py:142
  93.5 1.2 gather_fusion.5
  94.7 5.2 %all-to-all-done.3 = bf16[8,8,8]{2,1,0:T(8,128)(2,1)S(1)} async-done(((bf16[8,8,8]{2,1,0:T(8,128)(2,1)}), bf16[8,8,8]{2,1,0:T(8,128)(2,1)S(1)}, u32[]{:S(2)}, u32[]{:S(2)}) %all-to-all-start.3) | async-done | bytes 1056 | tf_op jit(solution)/shard_map/all_to_all | solution.py:142
  99.9 3.3 %all-to-all-start.4 = ((bf16[8,8,8]{2,1,0:T(8,128)(2,1)}), bf16[8,8,8]{2,1,0:T(8,128)(2,1)S(1)}, u32[]{:S(2)}, u32[]{:S(2)}) async-start(bf16[8,8,8]{2,1,0:T(8,128)(2,1)} %bitcast.64), calls=%async_computation.4 | async-start | bytes 32768 | tf_op jit(solution)/shard_map/all_to_all | solution.py:143
  103.3 1.3 gather_fusion.1
  104.6 0.6 gather_fusion.4
  105.2 4.5 %all-to-all-done.4 = bf16[8,8,8]{2,1,0:T(8,128)(2,1)S(1)} async-done(((bf16[8,8,8]{2,1,0:T(8,128)(2,1)}), bf16[8,8,8]{2,1,0:T(8,128)(2,1)S(1)}, u32[]{:S(2)}, u32[]{:S(2)}) %all-to-all-start.4) | async-done | bytes 1056 | tf_op jit(solution)/shard_map/all_to_all | solution.py:143
  109.7 3.4 %all-to-all-start.2 = ((bf16[8,8,8,128]{3,2,1,0:T(8,128)(2,1)}), bf16[8,8,8,128]{3,2,1,0:T(8,128)(2,1)S(1)}, u32[]{:S(2)}, u32[]{:S(2)}) async-start(bf16[8,8,8,128]{3,2,1,0:T(8,128)(2,1)} %bitcast.18), calls=%async_computation.2 | async-start | bytes 262144 | tf_op jit(solution)/shard_map/all_to_all | solution.py:144
  113.2 0.6 gather_fusion.6
  114.4 6.0 %all-to-all-done.2 = bf16[8,8,8,128]{3,2,1,0:T(8,128)(2,1)S(1)} async-done(((bf16[8,8,8,128]{3,2,1,0:T(8,128)(2,1)}), bf16[8,8,8,128]{3,2,1,0:T(8,128)(2,1)S(1)}, u32[]{:S(2)}, u32[]{:S(2)}) %all-to-all-start.2) | async-done | bytes 131104 | tf_op jit(solution)/shard_map/all_to_all | solution.py:144
  120.4 0.6 gather_fusion.2
  121.0 0.3 fusion.23
  121.3 0.9 convolution_convert_fusion
  122.3 29.6 %all-reduce.2.cloned.1.call-done = bf16[64,1536]{1,0:T(8,128)(2,1)} async-done(((bf16[64,1536]{1,0:T(8,128)(2,1)}), bf16[64,1536]{1,0:T(8,128)(2,1)}) %all-reduce.2.cloned.1.call-update) | async-done | bytes 196624 | tf_op jit(solution)/shard_map/psum | solution.py:171
  151.8 1.6 %copy.131 = bf16[64,1536]{1,0:T(8,128)(2,1)} copy(bf16[64,1536]{1,0:T(8,128)(2,1)} %all-reduce.2.cloned.1.call-done) | data formatting | bytes 393216
  (54 shorter events, 2.7 us)
Async XLA Ops:
  6.5 114.8 %copy-start = (bf16[256,1536]{1,0:T(8,128)(2,1)S(1)}, bf16[256,1536]{1,0:T(8,128)(2,1)}, u32[]{:S(2)}) copy-start(bf16[256,1536]{1,0:T(8,128)(2,1)} %param.15) | copy-start | bytes 2359300
  9.9 37.0 %all-to-all-start = ((s32[8,8,2]{1,2,0:T(2,128)}), s32[8,8,2]{1,2,0:T(2,128)S(1)}, u32[]{:S(2)}, u32[]{:S(2)}) async-start(s32[8,8,2]{1,2,0:T(2,128)} %copy.68), calls=%async_computation | async-start | bytes 16384 | tf_op jit(solution)/shard_map/all_to_all | solution.py:97
  46.8 13.5 %all-to-all-start.1 = ((bf16[8,8,8,128]{3,2,1,0:T(8,128)(2,1)}), bf16[8,8,8,128]{3,2,1,0:T(8,128)(2,1)S(1)}, u32[]{:S(2)}, u32[]{:S(2)}) async-start(bf16[8,8,8,128]{3,2,1,0:T(8,128)(2,1)} %bitcast.9), calls=%async_computation.1 | async-start | bytes 262144 | tf_op jit(solution)/shard_map/all_to_all | solution.py:111
  90.0 9.9 %all-to-all-start.3 = ((bf16[8,8,8]{2,1,0:T(8,128)(2,1)}), bf16[8,8,8]{2,1,0:T(8,128)(2,1)S(1)}, u32[]{:S(2)}, u32[]{:S(2)}) async-start(bf16[8,8,8]{2,1,0:T(8,128)(2,1)} %bitcast.65), calls=%async_computation.3 | async-start | bytes 32768 | tf_op jit(solution)/shard_map/all_to_all | solution.py:142
  99.9 9.9 %all-to-all-start.4 = ((bf16[8,8,8]{2,1,0:T(8,128)(2,1)}), bf16[8,8,8]{2,1,0:T(8,128)(2,1)S(1)}, u32[]{:S(2)}, u32[]{:S(2)}) async-start(bf16[8,8,8]{2,1,0:T(8,128)(2,1)} %bitcast.64), calls=%async_computation.4 | async-start | bytes 32768 | tf_op jit(solution)/shard_map/all_to_all | solution.py:143
  109.7 10.7 %all-to-all-start.2 = ((bf16[8,8,8,128]{3,2,1,0:T(8,128)(2,1)}), bf16[8,8,8,128]{3,2,1,0:T(8,128)(2,1)S(1)}, u32[]{:S(2)}, u32[]{:S(2)}) async-start(bf16[8,8,8,128]{3,2,1,0:T(8,128)(2,1)} %bitcast.18), calls=%async_computation.2 | async-start | bytes 262144 | tf_op jit(solution)/shard_map/all_to_all | solution.py:144
  113.1 38.7 %all-reduce.2.cloned.1.call-start = ((), (), s32[]{:S(2)}) async-start(), calls=%async_computation.5 | async-start | bytes 393216 | tf_op jit(solution)/shard_map/psum | solution.py:171
Sparse Core Ops, SparseCore 0:
  122.4 29.3 all-reduce.1
where the time goes:
time: 161 us; the launch traced here: 160 us
  waiting for transfers between devices  51.7 us (32%)
  local copies, waits for them, and re-layouts  31.7 us (20%)
  starting transfers between devices  23.4 us (15%)
  blocking collectives  23 us (14%)
  between operations  13.6 us (8%)
  matrix products  10.6 us (7%)
  other arithmetic  6.19 us (4%)
    psum x1, waiting for transfers between devices, local(): return lax.psum(partial_out.astype(jnp.bfloat16), 'tensor')  29.6 us
    all_gather x3, blocking collectives, combined_all(): lax.all_gather(a.astype(kind), axis)  17.6 us
    gather x1, local copies, waits for them, and re-layouts, local(): kv_pool[page_table].reshape(row_count, page_rows * page_len, 2 * head_width)  9.96 us
    scatter x2, local copies, waits for them, and re-layouts, to_buffer(): filled = empty.at[place].set(values)  7.66 us
    all_to_all x1, starting transfers between devices, local(): lax.all_to_all(tags, 'dp', split_axis=0, concat_axis=0, tiled=True)  7.28 us
    all_to_all x1, waiting for transfers between devices, local(): lax.all_to_all(to_buffer(full_query), 'dp', split_axis=0, concat_axis=0,...  6.47 us
    all_to_all x1, waiting for transfers between devices, local(): lax.all_to_all(as_sent(expand(merged[2])), 'dp', split_axis=0, concat_axi...  6.01 us
    all_to_all x1, starting transfers between devices, local(): lax.all_to_all(to_buffer(full_query), 'dp', split_axis=0, concat_axis=0,...  6 us
  transfers between devices with their start and end apart: 6, of which 5 were waited for; matrix products, arithmetic and copies ran while one was open for 19% of the time, Pallas kernels for 0%

commit v1 on v0

v1 whole, which is shorter than its diff:
```python
import functools

import jax
import jax.numpy as jnp
from jax import lax
from jax.experimental import pallas as pl
from jax.experimental.pallas import tpu as pltpu
from jax.sharding import PartitionSpec as P

masked_score = -1e30
peak_floor = -1e29
norm_eps = 1e-06
rotary_base = 10000.0
chunks = 8
MESH = pl.DeviceIdType.MESH
f32 = jnp.float32
bf16 = jnp.bfloat16


def dot(a, b):
    return jnp.dot(a, b, preferred_element_type=f32)


def dot_t(a, b):
    return lax.dot_general(a, b, (((1,), (1,)), ((), ())), preferred_element_type=f32)


def dot_exact(a, b):
    return jnp.dot(a, b, preferred_element_type=f32, precision=lax.Precision.HIGHEST)


def iota(shape, axis):
    return lax.broadcasted_iota(jnp.int32, shape, axis)


def split(values):
    high = values.astype(bf16).astype(f32)
    rest = values - high
    middle = rest.astype(bf16).astype(f32)
    return high, middle, rest - middle


def kernel(
    n_dp,
    n_tensor,
    capacity,
    tokens_hbm,
    gain_ref,
    wq_hbm,
    wkv_hbm,
    wo_hbm,
    pool_hbm,
    table_ref,
    position_ref,
    assign_ref,
    freq_ref,
    out_ref,
    tokens,
    wq,
    wkv,
    wo,
    pool,
    q_out,
    meta_out,
    q_in,
    meta_in,
    page_q,
    page_s,
    page_acc,
    stat_out,
    stat_in,
    sum_out,
    sum_in,
    load_sem,
    pool_sem,
    send_sem,
    recv_sem,
):
    dp = lax.axis_index("dp")
    tp = lax.axis_index("tensor")
    n_all = n_dp * n_tensor
    me = tp * n_dp + dp
    rows = tokens.shape[0]
    slots = n_dp * capacity
    width = wkv.shape[1] // 2
    half = width // 2
    local_heads = wq.shape[1] // width
    heads = local_heads * n_tensor
    pages, page_len = pool.shape[0], pool.shape[1]
    page_rows = table_ref.shape[1]
    window = page_rows * n_tensor * page_len
    chunk = pages // chunks
    scale = width ** (-0.5)
    out_rows = rows // n_tensor

    loads = [
        pltpu.make_async_copy(src, dst, load_sem.at[i])
        for i, (src, dst) in enumerate(
            ((tokens_hbm, tokens), (wq_hbm, wq), (wkv_hbm, wkv), (wo_hbm, wo))
        )
    ]
    for load in loads[:2]:
        load.start()

    barrier = pltpu.get_barrier_semaphore()

    def peer_of(i):
        other = lax.rem(me + i, n_all)
        return lax.rem(other, n_dp), lax.div(other, n_dp)

    @pl.loop(1, n_all)
    def _(i):
        pl.semaphore_signal(barrier, inc=1, device_id=peer_of(i), device_id_type=MESH)

    for load in loads[2:]:
        load.start()

    def pool_load(i):
        part = pl.ds(i * chunk, chunk)
        return pltpu.make_async_copy(pool_hbm.at[part], pool.at[part], pool_sem.at[i])

    for i in range(chunks):
        pool_load(i).start()

    eye = iota((rows, rows), 0) == iota((rows, rows), 1)
    before = iota((rows, rows), 1) < iota((rows, rows), 0)
    after = iota((rows, rows), 1) > iota((rows, rows), 0)

    def as_column(row):
        return jnp.sum(jnp.where(eye, row, 0.0), axis=1, keepdims=True)

    def as_row(column):
        return jnp.sum(jnp.where(eye, column, 0.0), axis=0, keepdims=True)

    position_row = position_ref[...].astype(f32)
    position = as_column(position_row)
    target_int = lax.div(assign_ref[...], rows)
    slot_row = (assign_ref[...] - target_int * rows).astype(f32)
    target_row = target_int.astype(f32)
    target = as_column(target_row)
    same = (target == target_row).astype(f32)
    place_row = target_row * capacity + jnp.sum(
        jnp.where(after, same, 0.0), axis=0, keepdims=True
    )
    place = target * capacity + jnp.sum(jnp.where(before, same, 0.0), axis=1, keepdims=True)
    to_place = iota((slots, rows), 0).astype(f32) == place_row
    from_place = (iota((rows, slots), 1).astype(f32) == place).astype(bf16)
    routed = to_place.astype(bf16)
    sent_position = jnp.sum(jnp.where(to_place, position_row, 0.0), axis=1, keepdims=True)
    sent_slot = jnp.sum(jnp.where(to_place, slot_row + 1.0, 0.0), axis=1, keepdims=True)
    high = jnp.floor(sent_position * (1.0 / 128.0))
    low = sent_position - high * 128.0
    lane = iota((slots, 128), 1)
    meta = jnp.where(lane == 0, high, jnp.where(lane == 1, low, jnp.where(lane == 2, sent_slot, 0.0)))
    meta_out[...] = meta.reshape(n_dp, capacity, 128).astype(bf16)

    angles = position * freq_ref[...]
    cosine = jnp.cos(angles)
    sine = jnp.sin(angles)

    def rotate(values):
        first, second = values[:, :half], values[:, half:]
        return jnp.concatenate(
            [first * cosine - second * sine, first * sine + second * cosine], axis=1
        )

    loads[0].wait()
    floats = tokens[...].astype(f32)
    normed = (
        floats
        * lax.rsqrt(jnp.mean(floats * floats, axis=-1, keepdims=True) + norm_eps)
        * gain_ref[...]
    ).astype(bf16)
    loads[1].wait()
    raw = dot(normed, wq[...])
    query = jnp.concatenate(
        [rotate(raw[:, h * width : (h + 1) * width]) for h in range(local_heads)], axis=1
    ).astype(bf16)
    q_out[...] = dot(routed, query).reshape(n_dp, capacity, local_heads * width).astype(bf16)

    pl.semaphore_wait(barrier, n_all - 1)

    def remote(src, dst, k, where):
        return pltpu.make_async_remote_copy(
            src_ref=src,
            dst_ref=dst,
            send_sem=send_sem.at[k],
            recv_sem=recv_sem.at[k],
            device_id=where,
            device_id_type=MESH,
        )

    def local_copy(src, dst, k):
        return pltpu.make_async_copy(src, dst, recv_sem.at[k])

    def wait_for(ref, sem):
        pltpu.make_async_copy(ref, ref, sem).wait()

    @pl.loop(1, n_dp)
    def _(i):
        d = lax.rem(dp + i, n_dp)
        remote(meta_out.at[d], meta_in.at[dp], 0, (d, tp)).start()

    local_copy(meta_out.at[dp], meta_in.at[dp], 0).start()

    @pl.loop(1, n_all)
    def _(i):
        d, t = peer_of(i)
        remote(q_out.at[d], q_in.at[me], 1, (d, t)).start()

    local_copy(q_out.at[dp], q_in.at[me], 1).start()

    loads[2].wait()
    key_value = dot(normed, wkv[...])
    new_key = rotate(key_value[:, :width]).astype(bf16).astype(f32)
    new_value = key_value[:, width:].astype(bf16).astype(f32)
    self_scores = [
        jnp.sum(
            query[:, h * width : (h + 1) * width].astype(f32) * new_key, axis=1, keepdims=True
        )
        * scale
        for h in range(local_heads)
    ]

    table = table_ref[...].astype(f32)
    page_id = iota((pages, rows), 0).astype(f32)
    holds = [(page_id == as_row(table[:, j : j + 1])).astype(f32) for j in range(page_rows)]
    first_page = holds[0].astype(bf16)
    any_page = sum(holds).astype(bf16)
    which = sum(j * jnp.sum(holds[j], axis=1, keepdims=True) for j in range(page_rows))
    swap = dot_t(any_page, any_page)
    swap = jnp.where(iota((pages, pages), 0) == iota((pages, pages), 1), 0.0, swap)
    key_slot = (tp * page_rows * page_len).astype(f32) + which * page_len + iota(
        (pages, page_len), 1
    ).astype(f32)

    wait_for(meta_in, recv_sem.at[0])
    got = meta_in[...].astype(f32).reshape(slots, 128)
    serves = (got[:, 2:3] - 1.0 == iota((slots, rows), 1).astype(f32)).astype(bf16)
    to_page = dot_t(any_page, serves).astype(bf16)
    from_page = dot_t(serves, any_page).astype(bf16)
    from_first = dot_t(serves, first_page)
    page_meta = dot(to_page, got.astype(bf16))
    page_position = page_meta[:, 0:1] * 128.0 + page_meta[:, 1:2]
    gap = key_slot - page_position
    offset = gap - window * jnp.floor(gap * (1.0 / window))
    live = (offset != 0.0) & (page_position - window + offset >= 0.0)
    mask = jnp.where(live, 0.0, masked_score)

    wait_for(q_in, recv_sem.at[1])
    for t in range(n_tensor):
        part = q_in[t * n_dp : (t + 1) * n_dp].astype(f32).reshape(slots, local_heads * width)
        spread = dot(to_page, part.astype(bf16))
        for h in range(local_heads):
            page_q[pl.ds(t * local_heads + h, pages, stride=heads), :] = spread[
                :, h * width : (h + 1) * width
            ]

    for i in range(chunks):
        pool_load(i).wait()

    pairs = pages // 2
    unroll = 8

    @pl.loop(0, pairs // unroll)
    def _(step):
        for u in range(unroll):
            pair = step * unroll + u
            at = pl.multiple_of(pair * 2 * heads, 2 * heads)
            keys = pool[pl.ds(pair * 2, 2), :, :width].reshape(2 * page_len, width)
            scores = dot_t(page_q[pl.ds(at, 2 * heads), :].astype(bf16), keys)
            page_s[pl.ds(at, heads), :] = scores[:heads, :page_len]
            page_s[pl.ds(at + heads, heads), :] = scores[heads:, page_len:]

    lanes = lax.rem(iota((pages, 128), 1), heads)
    peaks = jnp.zeros((pages, 128), f32)
    for h in range(heads):
        scored = page_s[pl.ds(h, pages, stride=heads), :] * scale + mask
        top = jnp.max(scored, axis=1, keepdims=True)
        peaks = jnp.where(lanes == h, top, peaks)
    peaks = jnp.maximum(peaks, peak_floor)
    peaks = jnp.maximum(peaks, dot_exact(swap, peaks))
    totals = jnp.zeros((pages, 128), f32)
    for h in range(heads):
        scored = page_s[pl.ds(h, pages, stride=heads), :] * scale + mask
        weight = jnp.exp(scored - peaks[:, h : h + 1])
        totals = jnp.where(lanes == h, jnp.sum(weight, axis=1, keepdims=True), totals)
        page_s[pl.ds(h, pages, stride=heads), :] = weight

    upper = iota((2 * heads, page_len), 0) < heads

    @pl.loop(0, pairs // unroll)
    def _(step):
        for u in range(unroll):
            pair = step * unroll + u
            at = pl.multiple_of(pair * 2 * heads, 2 * heads)
            weight = page_s[pl.ds(at, 2 * heads), :]
            both = jnp.concatenate(
                [jnp.where(upper, weight, 0.0), jnp.where(upper, 0.0, weight)], axis=1
            ).astype(bf16)
            values = pool[pl.ds(pair * 2, 2), :, width:].reshape(2 * page_len, width)
            page_acc[pl.ds(at, 2 * heads), :] = dot(both, values)

    own_peak = split(dot_exact(from_first, peaks))
    own_total = split(dot_exact(from_page.astype(f32), totals))
    group = lax.div(iota((slots, 128), 1), heads)
    stats = jnp.zeros((slots, 128), f32)
    for k, piece in enumerate(own_peak + own_total):
        stats = jnp.where(group == k, piece, stats)
    stats = stats.reshape(n_dp, capacity, 128).astype(bf16)
    for t in range(n_tensor):
        for h in range(local_heads):
            summed = page_acc[pl.ds(t * local_heads + h, pages, stride=heads), :].astype(bf16)
            stat_out[t * n_dp : (t + 1) * n_dp, :, h * width : (h + 1) * width] = (
                dot(from_page, summed).reshape(n_dp, capacity, width).astype(bf16)
            )
        stat_out[t * n_dp : (t + 1) * n_dp, :, local_heads * width :] = stats

    @pl.loop(1, n_all)
    def _(i):
        d, t = peer_of(i)
        remote(stat_out.at[t * n_dp + d], stat_in.at[me], 2, (d, t)).start()

    local_copy(stat_out.at[me], stat_in.at[me], 2).start()

    loads[3].wait()
    wait_for(stat_in, recv_sem.at[2])
    parts = []
    for t in range(n_tensor):
        part = stat_in[t * n_dp : (t + 1) * n_dp].astype(f32).reshape(slots, stat_in.shape[2])
        parts.append(dot(from_place, part.astype(bf16)))
    row_lane = iota((rows, 128), 1)
    row_head = lax.rem(row_lane, heads)
    row_group = lax.div(row_lane, heads)
    attended = []
    for h in range(local_heads):
        mine = row_head == tp * local_heads + h
        is_peak = mine & (row_group < 3)
        is_total = mine & (row_group >= 3) & (row_group < 6)
        tops, sums = [], []
        for part in parts:
            stat = part[:, local_heads * width :]
            tops.append(jnp.sum(jnp.where(is_peak, stat, 0.0), axis=1, keepdims=True))
            sums.append(jnp.sum(jnp.where(is_total, stat, 0.0), axis=1, keepdims=True))
        overall = functools.reduce(jnp.maximum, tops, self_scores[h])
        fresh = jnp.exp(self_scores[h] - overall)
        total = fresh
        acc = fresh.astype(bf16).astype(f32) * new_value
        for top, add, part in zip(tops, sums, parts):
            keep = jnp.exp(top - overall)
            total = total + add * keep
            acc = acc + part[:, h * width : (h + 1) * width] * keep
        attended.append(acc / total)
    attended = jnp.concatenate(attended, axis=1).astype(bf16)
    partial = dot(attended, wo[...])
    sum_out[...] = partial.reshape(n_tensor, out_rows, partial.shape[1]).astype(bf16)

    @pl.loop(1, n_tensor)
    def _(i):
        t = lax.rem(tp + i, n_tensor)
        remote(sum_out.at[t], sum_in.at[tp], 3, (dp, t)).start()

    local_copy(sum_out.at[tp], sum_in.at[tp], 3).start()
    wait_for(sum_in, recv_sem.at[3])
    done = sum_in[0].astype(f32)
    for t in range(1, n_tensor):
        done = done + sum_in[t].astype(f32)
    out_ref[tp] = done.astype(bf16)

    @pl.loop(1, n_tensor)
    def _(i):
        t = lax.rem(tp + i, n_tensor)
        remote(out_ref.at[tp], out_ref.at[tp], 4, (dp, t)).start()

    wait_for(out_ref.at[pl.ds(0, n_tensor - 1)], recv_sem.at[4])
    wait_for(meta_in.at[pl.ds(0, n_dp - 1)], send_sem.at[0])
    wait_for(q_in.at[pl.ds(0, n_all - 1)], send_sem.at[1])
    wait_for(stat_in.at[pl.ds(0, n_all - 1)], send_sem.at[2])
    wait_for(sum_in.at[pl.ds(0, n_tensor - 1)], send_sem.at[3])
    wait_for(out_ref.at[pl.ds(0, n_tensor - 1)], send_sem.at[4])


def local(tokens, norm_gain, w_query, w_keyval, w_out, kv_pool, page_table, positions, assignment):
    n_dp, n_tensor = lax.axis_size("dp"), lax.axis_size("tensor")
    rows, model = tokens.shape
    width = w_keyval.shape[1] // 2
    query_width = w_query.shape[1]
    heads = query_width // width * n_tensor
    capacity = max(8, rows // n_dp)
    n_all = n_dp * n_tensor
    pages = kv_pool.shape[0]
    half = width // 2
    freqs = rotary_base ** (-jnp.arange(half, dtype=f32) * 2.0 / width)
    whole = pl.BlockSpec(memory_space=pltpu.VMEM)
    anywhere = pl.BlockSpec(memory_space=pl.ANY)
    out = pl.pallas_call(
        functools.partial(kernel, n_dp, n_tensor, capacity),
        out_shape=jax.ShapeDtypeStruct((n_tensor, rows // n_tensor, model), bf16),
        in_specs=[anywhere, whole] + [anywhere] * 4 + [whole] * 4,
        out_specs=whole,
        scratch_shapes=[
            pltpu.VMEM(tokens.shape, bf16),
            pltpu.VMEM(w_query.shape, bf16),
            pltpu.VMEM(w_keyval.shape, bf16),
            pltpu.VMEM(w_out.shape, bf16),
            pltpu.VMEM(kv_pool.shape, bf16),
            pltpu.VMEM((n_dp, capacity, query_width), bf16),
            pltpu.VMEM((n_dp, capacity, 128), bf16),
            pltpu.VMEM((n_all, capacity, query_width), bf16),
            pltpu.VMEM((n_dp, capacity, 128), bf16),
            pltpu.VMEM((pages * heads, width), f32),
            pltpu.VMEM((pages * heads, kv_pool.shape[1]), f32),
            pltpu.VMEM((pages * heads, width), f32),
            pltpu.VMEM((n_all, capacity, query_width + 128), bf16),
            pltpu.VMEM((n_all, capacity, query_width + 128), bf16),
            pltpu.VMEM((n_tensor, rows // n_tensor, model), bf16),
            pltpu.VMEM((n_tensor, rows // n_tensor, model), bf16),
            pltpu.SemaphoreType.DMA((4,)),
            pltpu.SemaphoreType.DMA((chunks,)),
            pltpu.SemaphoreType.DMA((5,)),
            pltpu.SemaphoreType.DMA((5,)),
        ],
        compiler_params=pltpu.CompilerParams(
            collective_id=0, has_side_effects=True, vmem_limit_bytes=48 << 20
        ),
    )(
        tokens,
        norm_gain.reshape(1, model),
        w_query,
        w_keyval,
        w_out,
        kv_pool,
        page_table,
        positions.reshape(1, rows),
        assignment.reshape(1, rows),
        freqs.reshape(1, half),
    )
    return out.reshape(rows, model)


def solution(mesh):
    return jax.shard_map(
        local,
        mesh=mesh,
        in_specs=(
            P("dp", None),
            P(),
            P(None, "tensor"),
            P(),
            P("tensor", None),
            P(("dp", "tensor"), None, None),
            P("dp", "tensor"),
            P("dp"),
            P("dp"),
        ),
        out_specs=P("dp", None),
        check_vma=False,
    )
```

time: 161 us -> 40.6 us (0.25)
  waiting for transfers between devices: 51.7 us -> 0 us
  Pallas kernels: 0 us -> 32.3 us
  local copies, waits for them, and re-layouts: 31.7 us -> 7.79 us
  starting transfers between devices: 23.4 us -> 0 us
  blocking collectives: 23 us -> 0 us
  between operations: 13.6 us -> 0.02 us
  matrix products: 10.6 us -> 0 us
  other arithmetic: 6.19 us -> 0.01 us
    pallas_call x0 -> x1, Pallas kernels: none -> 32.3 us  [local(): pl.pallas_call(functools.partial(kernel, n_dp, n_tensor, capacity), out_s...]
    psum x1 -> x0, waiting for transfers between devices: 29.6 us -> none  [local(): return lax.psum(partial_out.astype(jnp.bfloat16), 'tensor')]
    all_to_all x5 -> x0, starting transfers between devices: 23.3 us -> none  [the longest x1 7.28 us: local(): lax.all_to_all(tags, 'dp', split_axis=0, concat_axis=0, tiled=True)]
    all_gather x4 -> x0, blocking collectives: 23 us -> none  [the longest x3 17.6 us: combined_all(): lax.all_gather(a.astype(kind), axis)]
    all_to_all x5 -> x0, waiting for transfers between devices: 22.2 us -> none  [the longest x1 6.47 us: local(): lax.all_to_all(to_buffer(full_query), 'dp', split_axis=0, concat_axis=0,...]
    gather x7 -> x0, local copies, waits for them, and re-layouts: 15.6 us -> none  [the longest x1 9.96 us: local(): kv_pool[page_table].reshape(row_count, page_rows * page_len, 2 * head_width)]
    scatter x4 -> x0, local copies, waits for them, and re-layouts: 10.9 us -> none  [the longest x2 7.66 us: to_buffer(): filled = empty.at[place].set(values)]
    dot_general x6 -> x0, matrix products: 10.6 us -> none  [the longest x1 3.45 us: local(): jnp.einsum('vto,vio->vti', served_heads, page_entries[..., :head_width],...]
  transfers between devices with their start and end apart: 6 -> 0, of which waited for: 5 -> 0; matrix products, arithmetic and copies ran while one was open for 19% -> 0% of each run, Pallas kernels for 0% -> 0%
where the time goes in v1:
time: 40.6 us; the launch traced here: 40.1 us
  Pallas kernels  32.3 us (80%)
  local copies, waits for them, and re-layouts  7.79 us (19%)
    pallas_call x1, Pallas kernels, local(): pl.pallas_call(functools.partial(kernel, n_dp, n_tensor, capacity), out_s...  32.3 us
    unnamed x14, local copies, waits for them, and re-layouts  7.08 us

profile of v1, /device:TPU:0, one launch (start us, length us, event | category | flops | bytes accessed | tf_op | source)
XLA Modules:
  0.0 40.1 jit_solution(15936772688573198019)
XLA Ops:
  0.0 0.7 %reshape.26.gain_ref = f32[1,1536]{1,0:T(1,128)S(1)} reshape(f32[1536]{0:T(1024)} %param.10) | data formatting | bytes 12288 | tf_op jit(solution)/shard_map/reshape | solution.py:428
  0.7 0.8 %copy.10.table_ref = s32[64,2]{1,0:T(8,128)S(1)} copy(s32[64,2]{0,1:T(2,128)} %param.15) | data formatting | bytes 1024 | tf_op args[6]
  1.5 0.0 copy-start
  1.5 1.1 %copy-done = bf16[1536,256]{1,0:T(8,128)(2,1)S(1)} copy-done((bf16[1536,256]{1,0:T(8,128)(2,1)S(1)}, bf16[1536,256]{1,0:T(8,128)(2,1)}, u32[]{:S(2)}) %copy-start) | copy-done | bytes 786456
  2.6 0.0 copy-start.1
  2.6 1.1 %copy-done.1 = bf16[1536,256]{1,0:T(8,128)(2,1)S(1)} copy-done((bf16[1536,256]{1,0:T(8,128)(2,1)S(1)}, bf16[1536,256]{1,0:T(8,128)(2,1)}, u32[]{:S(2)}) %copy-start.1) | copy-done | bytes 786456
  3.8 0.0 copy-start.2
  3.8 1.1 %copy-done.2 = bf16[256,1536]{1,0:T(8,128)(2,1)S(1)} copy-done((bf16[256,1536]{1,0:T(8,128)(2,1)S(1)}, bf16[256,1536]{1,0:T(8,128)(2,1)}, u32[]{:S(2)}) %copy-start.2) | copy-done | bytes 786456
  4.9 0.0 copy-start.3
  4.9 0.9 %copy-done.3 = bf16[64,1536]{1,0:T(8,128)(2,1)S(1)} copy-done((bf16[64,1536]{1,0:T(8,128)(2,1)S(1)}, bf16[64,1536]{1,0:T(8,128)(2,1)}, u32[]{:S(2)}) %copy-start.3) | copy-done | bytes 196632
  5.8 0.0 copy-start.4
  5.8 0.7 %copy-done.4 = s32[64]{0:T(128)S(1)} copy-done((s32[64]{0:T(128)S(1)}, s32[64]{0:T(128)}, u32[]{:S(2)}) %copy-start.4) | copy-done | bytes 280
  6.5 0.0 copy-start.5
  6.5 0.7 %copy-done.5 = s32[64]{0:T(128)S(1)} copy-done((s32[64]{0:T(128)S(1)}, s32[64]{0:T(128)}, u32[]{:S(2)}) %copy-start.5) | copy-done | bytes 280
  7.1 32.3 %shard_map.91 = bf16[4,16,1536]{2,1,0:T(8,128)(2,1)S(1)} custom-call(bf16[64,1536]{1,0:T(8,128)(2,1)S(1)} %copy-done.3, f32[1,1536]{1,0:T(1,128)S(1)} %reshape.26.gain_ref, bf16[1536,256]{1,0:T(8,128)(2,1)S(1)} %copy-done, bf16[1536,256]{1,0:T(8,128)(2,1)S(1)} %copy-done.1, bf16[256,1536]{1,0:T(8,128)(2,1)S(1)} %copy-done.2, ...), custom_call_target="tpu_custom_call" | custom-call | tf_op jit(solution)/shard_map/pallas_call | solution.py:396
  39.5 0.7 %copy.12 = bf16[64,1536]{1,0:T(8,128)(2,1)} copy(bf16[64,1536]{1,0:T(8,128)(2,1)S(1)} %bitcast.3) | data formatting | bytes 393216
  (1 shorter events, 0.0 us)
Async XLA Ops:
  1.5 1.1 %copy-start = (bf16[1536,256]{1,0:T(8,128)(2,1)S(1)}, bf16[1536,256]{1,0:T(8,128)(2,1)}, u32[]{:S(2)}) copy-start(bf16[1536,256]{1,0:T(8,128)(2,1)} %wq_hbm.1) | copy-start | bytes 2359300
  2.6 1.1 %copy-start.1 = (bf16[1536,256]{1,0:T(8,128)(2,1)S(1)}, bf16[1536,256]{1,0:T(8,128)(2,1)}, u32[]{:S(2)}) copy-start(bf16[1536,256]{1,0:T(8,128)(2,1)} %wkv_hbm.1) | copy-start | bytes 2359300
  3.8 1.1 %copy-start.2 = (bf16[256,1536]{1,0:T(8,128)(2,1)S(1)}, bf16[256,1536]{1,0:T(8,128)(2,1)}, u32[]{:S(2)}) copy-start(bf16[256,1536]{1,0:T(8,128)(2,1)} %wo_hbm.1) | copy-start | bytes 2359300
  4.9 0.9 %copy-start.3 = (bf16[64,1536]{1,0:T(8,128)(2,1)S(1)}, bf16[64,1536]{1,0:T(8,128)(2,1)}, u32[]{:S(2)}) copy-start(bf16[64,1536]{1,0:T(8,128)(2,1)} %tokens_hbm.1) | copy-start | bytes 589828
  5.8 0.7 %copy-start.4 = (s32[64]{0:T(128)S(1)}, s32[64]{0:T(128)}, u32[]{:S(2)}) copy-start(s32[64]{0:T(128)} %param.16) | copy-start | bytes 772
  6.5 0.7 %copy-start.5 = (s32[64]{0:T(128)S(1)}, s32[64]{0:T(128)}, u32[]{:S(2)}) copy-start(s32[64]{0:T(128)} %param.17) | copy-start | bytes 772

commit v2 on v1

--- a/solution.py
+++ b/solution.py
@@ -1,4 +1,5 @@
 import functools
+import math
 
 import jax
 import jax.numpy as jnp
@@ -45,17 +46,20 @@
     n_tensor,
     capacity,
     tokens_hbm,
-    gain_ref,
+    gain_hbm,
     wq_hbm,
     wkv_hbm,
     wo_hbm,
     pool_hbm,
+    table_hbm,
+    position_hbm,
+    assign_hbm,
+    out_ref,
+    tokens,
+    gain_ref,
     table_ref,
     position_ref,
     assign_ref,
-    freq_ref,
-    out_ref,
-    tokens,
     wq,
     wkv,
     wo,
@@ -87,7 +91,7 @@
     local_heads = wq.shape[1] // width
     heads = local_heads * n_tensor
     pages, page_len = pool.shape[0], pool.shape[1]
-    page_rows = table_ref.shape[1]
+    page_rows = table_ref.shape[0]
     window = page_rows * n_tensor * page_len
     chunk = pages // chunks
     scale = width ** (-0.5)
@@ -96,10 +100,19 @@
     loads = [
         pltpu.make_async_copy(src, dst, load_sem.at[i])
         for i, (src, dst) in enumerate(
-            ((tokens_hbm, tokens), (wq_hbm, wq), (wkv_hbm, wkv), (wo_hbm, wo))
+            (
+                (position_hbm, position_ref),
+                (assign_hbm, assign_ref),
+                (tokens_hbm, tokens),
+                (gain_hbm, gain_ref),
+                (wq_hbm, wq),
+                (table_hbm, table_ref),
+                (wkv_hbm, wkv),
+                (wo_hbm, wo),
+            )
         )
     ]
-    for load in loads[:2]:
+    for load in loads[:5]:
         load.start()
 
     barrier = pltpu.get_barrier_semaphore()
@@ -112,7 +125,7 @@
     def _(i):
         pl.semaphore_signal(barrier, inc=1, device_id=peer_of(i), device_id_type=MESH)
 
-    for load in loads[2:]:
+    for load in loads[5:]:
         load.start()
 
     def pool_load(i):
@@ -129,9 +142,8 @@
     def as_column(row):
         return jnp.sum(jnp.where(eye, row, 0.0), axis=1, keepdims=True)
 
-    def as_row(column):
-        return jnp.sum(jnp.where(eye, column, 0.0), axis=0, keepdims=True)
-
+    loads[0].wait()
+    loads[1].wait()
     position_row = position_ref[...].astype(f32)
     position = as_column(position_row)
     target_int = lax.div(assign_ref[...], rows)
@@ -154,7 +166,8 @@
     meta = jnp.where(lane == 0, high, jnp.where(lane == 1, low, jnp.where(lane == 2, sent_slot, 0.0)))
     meta_out[...] = meta.reshape(n_dp, capacity, 128).astype(bf16)
 
-    angles = position * freq_ref[...]
+    step = -2.0 * math.log(rotary_base) / width
+    angles = position * jnp.exp(iota((1, half), 1).astype(f32) * step)
     cosine = jnp.cos(angles)
     sine = jnp.sin(angles)
 
@@ -164,14 +177,16 @@
             [first * cosine - second * sine, first * sine + second * cosine], axis=1
         )
 
-    loads[0].wait()
+    loads[2].wait()
+    loads[3].wait()
+    gain = jnp.concatenate([gain_ref[i : i + 1, :] for i in range(gain_ref.shape[0])], axis=1)
     floats = tokens[...].astype(f32)
     normed = (
         floats
         * lax.rsqrt(jnp.mean(floats * floats, axis=-1, keepdims=True) + norm_eps)
-        * gain_ref[...]
+        * gain
     ).astype(bf16)
-    loads[1].wait()
+    loads[4].wait()
     raw = dot(normed, wq[...])
     query = jnp.concatenate(
         [rotate(raw[:, h * width : (h + 1) * width]) for h in range(local_heads)], axis=1
@@ -210,7 +225,7 @@
 
     local_copy(q_out.at[dp], q_in.at[me], 1).start()
 
-    loads[2].wait()
+    loads[6].wait()
     key_value = dot(normed, wkv[...])
     new_key = rotate(key_value[:, :width]).astype(bf16).astype(f32)
     new_value = key_value[:, width:].astype(bf16).astype(f32)
@@ -222,9 +237,10 @@
         for h in range(local_heads)
     ]
 
+    loads[5].wait()
     table = table_ref[...].astype(f32)
     page_id = iota((pages, rows), 0).astype(f32)
-    holds = [(page_id == as_row(table[:, j : j + 1])).astype(f32) for j in range(page_rows)]
+    holds = [(page_id == table[j : j + 1, :]).astype(f32) for j in range(page_rows)]
     first_page = holds[0].astype(bf16)
     any_page = sum(holds).astype(bf16)
     which = sum(j * jnp.sum(holds[j], axis=1, keepdims=True) for j in range(page_rows))
@@ -323,7 +339,7 @@
 
     local_copy(stat_out.at[me], stat_in.at[me], 2).start()
 
-    loads[3].wait()
+    loads[7].wait()
     wait_for(stat_in, recv_sem.at[2])
     parts = []
     for t in range(n_tensor):
@@ -389,17 +405,19 @@
     capacity = max(8, rows // n_dp)
     n_all = n_dp * n_tensor
     pages = kv_pool.shape[0]
-    half = width // 2
-    freqs = rotary_base ** (-jnp.arange(half, dtype=f32) * 2.0 / width)
     whole = pl.BlockSpec(memory_space=pltpu.VMEM)
-    anywhere = pl.BlockSpec(memory_space=pl.ANY)
+    far = pl.BlockSpec(memory_space=pltpu.HBM)
     out = pl.pallas_call(
         functools.partial(kernel, n_dp, n_tensor, capacity),
         out_shape=jax.ShapeDtypeStruct((n_tensor, rows // n_tensor, model), bf16),
-        in_specs=[anywhere, whole] + [anywhere] * 4 + [whole] * 4,
+        in_specs=[far] * 9,
         out_specs=whole,
         scratch_shapes=[
             pltpu.VMEM(tokens.shape, bf16),
+            pltpu.VMEM((model // 128, 128), f32),
+            pltpu.VMEM(page_table.shape[::-1], jnp.int32),
+            pltpu.VMEM((1, rows), jnp.int32),
+            pltpu.VMEM((1, rows), jnp.int32),
             pltpu.VMEM(w_query.shape, bf16),
             pltpu.VMEM(w_keyval.shape, bf16),
             pltpu.VMEM(w_out.shape, bf16),
@@ -415,25 +433,24 @@
             pltpu.VMEM((n_all, capacity, query_width + 128), bf16),
             pltpu.VMEM((n_tensor, rows // n_tensor, model), bf16),
             pltpu.VMEM((n_tensor, rows // n_tensor, model), bf16),
-            pltpu.SemaphoreType.DMA((4,)),
+            pltpu.SemaphoreType.DMA((8,)),
             pltpu.SemaphoreType.DMA((chunks,)),
             pltpu.SemaphoreType.DMA((5,)),
             pltpu.SemaphoreType.DMA((5,)),
         ],
         compiler_params=pltpu.CompilerParams(
-            collective_id=0, has_side_effects=True, vmem_limit_bytes=48 << 20
+            collective_id=0, has_side_effects=True, vmem_limit_bytes=62 << 20
         ),
     )(
         tokens,
-        norm_gain.reshape(1, model),
+        norm_gain.reshape(model // 128, 128),
         w_query,
         w_keyval,
         w_out,
         kv_pool,
-        page_table,
+        page_table.T,
         positions.reshape(1, rows),
         assignment.reshape(1, rows),
-        freqs.reshape(1, half),
     )
     return out.reshape(rows, model)
 

time: 40.6 us -> 34.6 us (0.85)
  local copies, waits for them, and re-layouts: 7.79 us -> 1.62 us
    unnamed x14 -> x1, local copies, waits for them, and re-layouts: 7.08 us -> 1.62 us
    reshape x1 -> x0, local copies, waits for them, and re-layouts: 0.71 us -> none  [local(): norm_gain.reshape(1, model)]
where the time goes in v2:
time: 34.6 us; the launch traced here: 34.3 us
  Pallas kernels  32.7 us (95%)
  local copies, waits for them, and re-layouts  1.62 us (5%)
    pallas_call x1, Pallas kernels, local(): pl.pallas_call(functools.partial(kernel, n_dp, n_tensor, capacity), out_s...  32.7 us
    unnamed x1, local copies, waits for them, and re-layouts  1.62 us

profile of v2, /device:TPU:0, one launch (start us, length us, event | category | flops | bytes accessed | tf_op | source)
XLA Modules:
  0.0 34.3 jit_solution(16788989706325973864)
XLA Ops:
  0.0 32.7 %shard_map.91 = bf16[4,16,1536]{2,1,0:T(8,128)(2,1)} custom-call(bf16[64,1536]{1,0:T(8,128)(2,1)} %tokens_hbm.1, f32[12,128]{1,0:T(8,128)} %bitcast.6, bf16[1536,256]{1,0:T(8,128)(2,1)} %wq_hbm.1, bf16[1536,256]{1,0:T(8,128)(2,1)} %wkv_hbm.1, bf16[256,1536]{1,0:T(8,128)(2,1)} %wo_hbm.1, bf16[128,128,256]{2,1,0:T(8,128)(2,1)} %pool_hbm.1, s32[2,64]{1,0:T(2,128)} %bitcast.7, ...), custom_call_target="tpu_custom_call" | custom-call | tf_op jit(solution)/shard_map/pallas_call | solution.py:410
  32.7 1.6 %copy.11 = bf16[64,1536]{1,0:T(8,128)(2,1)} copy(bf16[64,1536]{1,0:T(8,128)(2,1)} %bitcast.5) | data formatting | bytes 393216

commit v3 on v2

--- a/solution.py
+++ b/solution.py
@@ -32,13 +32,6 @@
 
 def iota(shape, axis):
     return lax.broadcasted_iota(jnp.int32, shape, axis)
-
-
-def split(values):
-    high = values.astype(bf16).astype(f32)
-    rest = values - high
-    middle = rest.astype(bf16).astype(f32)
-    return high, middle, rest - middle
 
 
 def kernel(
@@ -73,8 +66,11 @@
     page_acc,
     stat_out,
     stat_in,
+    small_out,
+    small_in,
     sum_out,
     sum_in,
+    pair_sum,
     load_sem,
     pool_sem,
     send_sem,
@@ -317,47 +313,57 @@
             values = pool[pl.ds(pair * 2, 2), :, width:].reshape(2 * page_len, width)
             page_acc[pl.ds(at, 2 * heads), :] = dot(both, values)
 
-    own_peak = split(dot_exact(from_first, peaks))
-    own_total = split(dot_exact(from_page.astype(f32), totals))
-    group = lax.div(iota((slots, 128), 1), heads)
-    stats = jnp.zeros((slots, 128), f32)
-    for k, piece in enumerate(own_peak + own_total):
-        stats = jnp.where(group == k, piece, stats)
-    stats = stats.reshape(n_dp, capacity, 128).astype(bf16)
+    own_peak = dot_exact(from_first, peaks)
+    own_total = dot_exact(from_page.astype(f32), totals)
+    packed = lax.div(iota((slots, 128), 1), heads)
+    within = lax.rem(iota((slots, 128), 0), capacity)
+    stats = jnp.where(
+        packed == within, own_peak, jnp.where(packed == within + capacity, own_total, 0.0)
+    )
+    small_out[...] = jnp.sum(stats.reshape(n_dp, capacity, 128), axis=1, keepdims=True)
     for t in range(n_tensor):
         for h in range(local_heads):
             summed = page_acc[pl.ds(t * local_heads + h, pages, stride=heads), :].astype(bf16)
             stat_out[t * n_dp : (t + 1) * n_dp, :, h * width : (h + 1) * width] = (
                 dot(from_page, summed).reshape(n_dp, capacity, width).astype(bf16)
             )
-        stat_out[t * n_dp : (t + 1) * n_dp, :, local_heads * width :] = stats
 
     @pl.loop(1, n_all)
     def _(i):
         d, t = peer_of(i)
+        remote(small_out.at[d], small_in.at[me], 5, (d, t)).start()
         remote(stat_out.at[t * n_dp + d], stat_in.at[me], 2, (d, t)).start()
 
+    local_copy(small_out.at[dp], small_in.at[me], 5).start()
     local_copy(stat_out.at[me], stat_in.at[me], 2).start()
 
     loads[7].wait()
     wait_for(stat_in, recv_sem.at[2])
-    parts = []
+    wait_for(small_in, recv_sem.at[5])
+    parts, heads_of = [], []
+    row_lane = iota((slots, 128), 1)
+    row_head = lax.rem(row_lane, heads)
+    row_place = lax.div(row_lane, heads)
+    row_within = lax.rem(iota((slots, 128), 0), capacity)
     for t in range(n_tensor):
-        part = stat_in[t * n_dp : (t + 1) * n_dp].astype(f32).reshape(slots, stat_in.shape[2])
+        part = stat_in[t * n_dp : (t + 1) * n_dp].astype(f32).reshape(slots, local_heads * width)
         parts.append(dot(from_place, part.astype(bf16)))
-    row_lane = iota((rows, 128), 1)
-    row_head = lax.rem(row_lane, heads)
-    row_group = lax.div(row_lane, heads)
+        small = jnp.broadcast_to(
+            small_in[t * n_dp : (t + 1) * n_dp], (n_dp, capacity, 128)
+        ).reshape(slots, 128)
+        columns = jnp.zeros((slots, 128), f32)
+        for h in range(local_heads):
+            mine = row_head == tp * local_heads + h
+            for k, at in enumerate((row_within, row_within + capacity)):
+                picked = jnp.sum(
+                    jnp.where(mine & (row_place == at), small, 0.0), axis=1, keepdims=True
+                )
+                columns = jnp.where(row_lane == 2 * h + k, picked, columns)
+        heads_of.append(dot_exact(from_place.astype(f32), columns))
     attended = []
     for h in range(local_heads):
-        mine = row_head == tp * local_heads + h
-        is_peak = mine & (row_group < 3)
-        is_total = mine & (row_group >= 3) & (row_group < 6)
-        tops, sums = [], []
-        for part in parts:
-            stat = part[:, local_heads * width :]
-            tops.append(jnp.sum(jnp.where(is_peak, stat, 0.0), axis=1, keepdims=True))
-            sums.append(jnp.sum(jnp.where(is_total, stat, 0.0), axis=1, keepdims=True))
+        tops = [column[:, 2 * h : 2 * h + 1] for column in heads_of]
+        sums = [column[:, 2 * h + 1 : 2 * h + 2] for column in heads_of]
         overall = functools.reduce(jnp.maximum, tops, self_scores[h])
         fresh = jnp.exp(self_scores[h] - overall)
         total = fresh
@@ -371,29 +377,25 @@
     partial = dot(attended, wo[...])
     sum_out[...] = partial.reshape(n_tensor, out_rows, partial.shape[1]).astype(bf16)
 
-    @pl.loop(1, n_tensor)
-    def _(i):
-        t = lax.rem(tp + i, n_tensor)
-        remote(sum_out.at[t], sum_in.at[tp], 3, (dp, t)).start()
-
-    local_copy(sum_out.at[tp], sum_in.at[tp], 3).start()
-    wait_for(sum_in, recv_sem.at[3])
-    done = sum_in[0].astype(f32)
-    for t in range(1, n_tensor):
-        done = done + sum_in[t].astype(f32)
-    out_ref[tp] = done.astype(bf16)
-
-    @pl.loop(1, n_tensor)
-    def _(i):
-        t = lax.rem(tp + i, n_tensor)
-        remote(out_ref.at[tp], out_ref.at[tp], 4, (dp, t)).start()
-
-    wait_for(out_ref.at[pl.ds(0, n_tensor - 1)], recv_sem.at[4])
+    parity = lax.rem(tp, 2)
+    sibling = tp + 1 - 2 * parity
+    opposite = lax.rem(tp + 2, n_tensor)
+    mine = pl.ds(2 * parity, 2)
+    theirs = pl.ds(2 - 2 * parity, 2)
+    remote(sum_out.at[theirs], sum_in.at[0:2], 3, (dp, sibling)).start()
+    wait_for(sum_in.at[0:2], recv_sem.at[3])
+    pair_sum[...] = (sum_out[mine].astype(f32) + sum_in[0:2].astype(f32)).astype(bf16)
+    remote(pair_sum, sum_in.at[2:4], 4, (dp, opposite)).start()
+    wait_for(sum_in.at[2:4], recv_sem.at[4])
+    out_ref[mine] = (pair_sum[...].astype(f32) + sum_in[2:4].astype(f32)).astype(bf16)
+    remote(out_ref.at[mine], out_ref.at[mine], 6, (dp, sibling)).start()
+    wait_for(out_ref.at[theirs], recv_sem.at[6])
     wait_for(meta_in.at[pl.ds(0, n_dp - 1)], send_sem.at[0])
     wait_for(q_in.at[pl.ds(0, n_all - 1)], send_sem.at[1])
     wait_for(stat_in.at[pl.ds(0, n_all - 1)], send_sem.at[2])
-    wait_for(sum_in.at[pl.ds(0, n_tensor - 1)], send_sem.at[3])
-    wait_for(out_ref.at[pl.ds(0, n_tensor - 1)], send_sem.at[4])
+    wait_for(small_in.at[pl.ds(0, n_all - 1)], send_sem.at[5])
+    for k in (3, 4, 6):
+        wait_for(pair_sum, send_sem.at[k])
 
 
 def local(tokens, norm_gain, w_query, w_keyval, w_out, kv_pool, page_table, positions, assignment):
@@ -429,14 +431,17 @@
             pltpu.VMEM((pages * heads, width), f32),
             pltpu.VMEM((pages * heads, kv_pool.shape[1]), f32),
             pltpu.VMEM((pages * heads, width), f32),
-            pltpu.VMEM((n_all, capacity, query_width + 128), bf16),
-            pltpu.VMEM((n_all, capacity, query_width + 128), bf16),
+            pltpu.VMEM((n_all, capacity, query_width), bf16),
+            pltpu.VMEM((n_all, capacity, query_width), bf16),
+            pltpu.VMEM((n_dp, 1, 128), f32),
+            pltpu.VMEM((n_all, 1, 128), f32),
             pltpu.VMEM((n_tensor, rows // n_tensor, model), bf16),
             pltpu.VMEM((n_tensor, rows // n_tensor, model), bf16),
+            pltpu.VMEM((2, rows // n_tensor, model), bf16),
             pltpu.SemaphoreType.DMA((8,)),
             pltpu.SemaphoreType.DMA((chunks,)),
-            pltpu.SemaphoreType.DMA((5,)),
-            pltpu.SemaphoreType.DMA((5,)),
+            pltpu.SemaphoreType.DMA((7,)),
+            pltpu.SemaphoreType.DMA((7,)),
         ],
         compiler_params=pltpu.CompilerParams(
             collective_id=0, has_side_effects=True, vmem_limit_bytes=62 << 20

time: 34.6 us -> 33 us (0.954)
  Pallas kernels: 32.7 us -> 31.3 us
    pallas_call x1, Pallas kernels: 32.7 us -> 31.3 us  [local(): pl.pallas_call(functools.partial(kernel, n_dp, n_tensor, capacity), out_s...]
where the time goes in v3:
time: 33 us; the launch traced here: 32.9 us
  Pallas kernels  31.3 us (95%)
  local copies, waits for them, and re-layouts  1.62 us (5%)
    pallas_call x1, Pallas kernels, local(): pl.pallas_call(functools.partial(kernel, n_dp, n_tensor, capacity), out_s...  31.3 us
    unnamed x1, local copies, waits for them, and re-layouts  1.62 us

profile of v3, /device:TPU:0, one launch (start us, length us, event | category | flops | bytes accessed | tf_op | source)
XLA Modules:
  0.0 32.9 jit_solution(16446508627628042898)
XLA Ops:
  0.0 31.3 %shard_map.91 = bf16[4,16,1536]{2,1,0:T(8,128)(2,1)} custom-call(bf16[64,1536]{1,0:T(8,128)(2,1)} %tokens_hbm.1, f32[12,128]{1,0:T(8,128)} %bitcast.6, bf16[1536,256]{1,0:T(8,128)(2,1)} %wq_hbm.1, bf16[1536,256]{1,0:T(8,128)(2,1)} %wkv_hbm.1, bf16[256,1536]{1,0:T(8,128)(2,1)} %wo_hbm.1, bf16[128,128,256]{2,1,0:T(8,128)(2,1)} %pool_hbm.1, s32[2,64]{1,0:T(2,128)} %bitcast.7, ...), custom_call_target="tpu_custom_call" | custom-call | tf_op jit(solution)/shard_map/pallas_call | solution.py:412
  31.3 1.6 %copy.11 = bf16[64,1536]{1,0:T(8,128)(2,1)} copy(bf16[64,1536]{1,0:T(8,128)(2,1)} %bitcast.5) | data formatting | bytes 393216
